TPU v7x, 32 devices: a whole 2x2x4 slice. The times are simulated.
32 devices in a mesh: rep: 4 (over y, x), shard: 8 (over z, core).
Axes of the slice: x: 2, y: 2, z: 4, core: 2. Of those that a mesh axis runs over, the one named last changes fastest.
Arguments:
- hidden_in: float32 [4096, 768], P(('rep', 'shard')), may hold values from -6 to 6
- doc_ids: int32 [32, 128], P(('rep', 'shard')), may hold values from 0 to 3, never falling along the last dimension, each value on 1 to 64 neighbouring positions
- cotangent: float32 [4096, 768], P(('rep', 'shard')), may hold values from -6 to 6
- pre_gain: float32 [1, 768], P(None, 'shard'), may hold values from 0.25 to 1.75
- pre_shift: float32 [1, 768], P(None, 'shard'), may hold values from -3 to 3
- qkv_weight: float32 [1, 768, 2304], P(None, 'shard'), may hold values from -0.21875 to 0.21875
- query_bias: float32 [1, 768], P(None, 'shard'), may hold values from -3 to 3
- value_bias: float32 [1, 768], P(None, 'shard'), may hold values from -3 to 3
- out_weight: float32 [1, 768, 768], P(None, 'shard'), may hold values from -0.875 to 0.875
- out_bias: float32 [1, 768], P(None, 'shard'), may hold values from -3 to 3
- post_gain: float32 [1, 768], P(None, 'shard'), may hold values from 0.25 to 1.75
- post_shift: float32 [1, 768], P(None, 'shard'), may hold values from -3 to 3
- up_weight: float32 [1, 768, 3072], P(None, 'shard'), may hold values from -0.21875 to 0.21875
- up_bias: float32 [1, 3072], P(None, 'shard'), may hold values from -3 to 3
- down_weight: float32 [1, 3072, 768], P(None, 'shard'), may hold values from -0.109375 to 0.109375
- down_bias: float32 [1, 768], P(None, 'shard'), may hold values from -3 to 3
Outputs:
- hidden_out: float32 [4096, 768], P(('rep', 'shard'))
- input_grad: float32 [4096, 768], P(('rep', 'shard'))
- grad_pre_gain: float32 [1, 768], P(None, 'shard')
- grad_pre_shift: float32 [1, 768], P(None, 'shard')
- grad_qkv_weight: float32 [1, 768, 2304], P(None, 'shard')
- grad_query_bias: float32 [1, 768], P(None, 'shard')
- grad_value_bias: float32 [1, 768], P(None, 'shard')
- grad_out_weight: float32 [1, 768, 768], P(None, 'shard')
- grad_out_bias: float32 [1, 768], P(None, 'shard')
- grad_post_gain: float32 [1, 768], P(None, 'shard')
- grad_post_shift: float32 [1, 768], P(None, 'shard')
- grad_up_weight: float32 [1, 768, 3072], P(None, 'shard')
- grad_up_bias: float32 [1, 3072], P(None, 'shard')
- grad_down_weight: float32 [1, 3072, 768], P(None, 'shard')
- grad_down_bias: float32 [1, 768], P(None, 'shard')
Inputs may be any that keep to these rules, and one draw needn't show every extreme that they name: `doc_ids`: along each row the document number never falls; all 4 documents appear in every row, each of 1 to 64 tokens, one of exactly 64.
All inputs are finite; a program needn't handle non-finite values.
Results may differ from a plain program's by a relative error of at most 0.018.
Values may be sent and summed in bfloat16 or wider, within the bound.
No kernel may reach another device: no remote copies, remote signals or barrier semaphores. Data moves between devices by JAX's collectives and lax.ppermute only.
A program may use at most 128 MiB of HBM per device.

v0:
```python
import jax
import jax.numpy as jnp
from jax import lax
from jax.sharding import PartitionSpec as P

HEADS = 12
HEAD = 64
LAYERS = 1
EPS = 1e-05
GELU_C = 0.7978845608028654
NEG_FILL = -1e30


def norm(values_in, gains, shifts):
    average = jnp.mean(values_in, axis=-1, keepdims=True)
    centred = values_in - average
    spread = jnp.mean(centred * centred, axis=-1, keepdims=True)
    return centred * lax.rsqrt(spread + EPS) * gains + shifts


def gelu_tanh(values_in):
    return (
        0.5
        * values_in
        * (1.0 + jnp.tanh(GELU_C * (values_in + 0.044715 * values_in * values_in * values_in)))
    )


def project(left, right):
    return jnp.dot(left, right, preferred_element_type=jnp.float32)


def project_back(left, right):
    return lax.dot_general(
        left, right, (((0,), (0,)), ((), ())), preferred_element_type=jnp.float32
    )


def project_trans(left, right):
    return lax.dot_general(
        left, right, (((1,), (1,)), ((), ())), preferred_element_type=jnp.float32
    )


def layer_slices(shards, layer_index):
    return tuple((stacked[layer_index].astype(jnp.bfloat16) for stacked in shards))


def fetch_forward(shards, layer_index):
    parts = layer_slices(shards, layer_index)
    return (
        lax.all_gather(parts[0], "shard", axis=0, tiled=True),
        lax.all_gather(parts[1], "shard", axis=0, tiled=True),
        lax.all_gather(parts[2], "shard", axis=0, tiled=True),
        lax.all_gather(parts[3], "shard", axis=0, tiled=True),
        lax.all_gather(parts[4], "shard", axis=0, tiled=True),
        lax.all_gather(parts[5], "shard", axis=0, tiled=True),
        lax.all_gather(parts[6], "shard", axis=0, tiled=True),
        lax.all_gather(parts[7], "shard", axis=0, tiled=True),
        lax.all_gather(parts[8], "shard", axis=0, tiled=True),
        lax.all_gather(parts[9], "shard", axis=0, tiled=True),
        lax.all_gather(parts[10], "shard", axis=0, tiled=True),
        lax.all_gather(parts[11], "shard", axis=0, tiled=True),
        lax.all_gather(parts[12], "shard", axis=0, tiled=True),
    )


def reduce_nested_rest(grads):
    owned = (
        lax.psum_scatter(
            grads[0].astype(jnp.bfloat16), "shard", scatter_dimension=0, tiled=True
        ).astype(jnp.float32),
        lax.psum_scatter(
            grads[1].astype(jnp.bfloat16), "shard", scatter_dimension=0, tiled=True
        ).astype(jnp.float32),
        lax.psum_scatter(
            grads[2].astype(jnp.bfloat16), "shard", scatter_dimension=0, tiled=True
        ).astype(jnp.float32),
        lax.psum_scatter(
            grads[3].astype(jnp.bfloat16), "shard", scatter_dimension=0, tiled=True
        ).astype(jnp.float32),
        lax.psum_scatter(
            grads[4].astype(jnp.bfloat16), "shard", scatter_dimension=0, tiled=True
        ).astype(jnp.float32),
        lax.psum_scatter(
            grads[5].astype(jnp.bfloat16), "shard", scatter_dimension=0, tiled=True
        ).astype(jnp.float32),
        lax.psum_scatter(
            grads[6].astype(jnp.bfloat16), "shard", scatter_dimension=0, tiled=True
        ).astype(jnp.float32),
        lax.psum_scatter(
            grads[7].astype(jnp.bfloat16), "shard", scatter_dimension=0, tiled=True
        ).astype(jnp.float32),
        lax.psum_scatter(
            grads[8].astype(jnp.bfloat16), "shard", scatter_dimension=0, tiled=True
        ).astype(jnp.float32),
        lax.psum_scatter(
            grads[9].astype(jnp.bfloat16), "shard", scatter_dimension=0, tiled=True
        ).astype(jnp.float32),
        lax.psum_scatter(
            grads[10].astype(jnp.bfloat16), "shard", scatter_dimension=0, tiled=True
        ).astype(jnp.float32),
    )
    return (
        lax.psum(owned[0].astype(jnp.bfloat16), "rep").astype(jnp.float32),
        lax.psum(owned[1].astype(jnp.bfloat16), "rep").astype(jnp.float32),
        lax.psum(owned[2].astype(jnp.bfloat16), "rep").astype(jnp.float32),
        lax.psum(owned[3].astype(jnp.bfloat16), "rep").astype(jnp.float32),
        lax.psum(owned[4].astype(jnp.bfloat16), "rep").astype(jnp.float32),
        lax.psum(owned[5].astype(jnp.bfloat16), "rep").astype(jnp.float32),
        lax.psum(owned[6].astype(jnp.bfloat16), "rep").astype(jnp.float32),
        lax.psum(owned[7].astype(jnp.bfloat16), "rep").astype(jnp.float32),
        lax.psum(owned[8].astype(jnp.bfloat16), "rep").astype(jnp.float32),
        lax.psum(owned[9].astype(jnp.bfloat16), "rep").astype(jnp.float32),
        lax.psum(owned[10].astype(jnp.bfloat16), "rep").astype(jnp.float32),
    )


def block_scores(query_block, key_rows, doc_block, doc_row, offset):
    query_places = offset + lax.iota(jnp.int32, query_block.shape[0])
    key_places = lax.iota(jnp.int32, key_rows.shape[0])
    allowed = (query_places[:, None] >= key_places[None, :]) & (
        doc_block[:, None] == doc_row[None, :]
    )
    scores = (
        jnp.einsum("qhe,khe->hqk", query_block, key_rows, preferred_element_type=jnp.float32)
        * 0.125
    )
    return jnp.where(allowed[None], scores, NEG_FILL)


def attention_forward(queries, key_rows, value_rows, doc_row):
    length = queries.shape[0]
    rows_block = min(length, 512)
    blocks = length // rows_block

    def one_block(block_index):
        offset = block_index * rows_block
        scores = block_scores(queries, key_rows, doc_row, doc_row, offset)
        highest = jnp.max(scores, axis=-1, keepdims=True)
        log_total = highest + jnp.log(jnp.sum(jnp.exp(scores - highest), axis=-1, keepdims=True))
        weights = jnp.exp(scores - log_total).astype(jnp.bfloat16)
        mixed = jnp.einsum("hqk,khe->qhe", weights, value_rows, preferred_element_type=jnp.float32)
        return (mixed.astype(jnp.bfloat16), log_total)

    mixed, log_totals = lax.map(one_block, jnp.arange(blocks, dtype=jnp.int32))
    return (mixed.reshape(length, -1), log_totals)


def attention_backward(queries, key_rows, value_rows, doc_row, log_totals, grad_mixed):
    length = queries.shape[0]
    rows_block = min(length, 512)
    blocks = length // rows_block

    def one_block(carry, block_index):
        grad_keys, grad_values = carry
        offset = block_index * rows_block
        scores = block_scores(queries, key_rows, doc_row, doc_row, offset)
        weights = jnp.exp(scores - log_totals[block_index])
        grad_values = grad_values + jnp.einsum(
            "hqk,qhe->khe",
            weights.astype(jnp.bfloat16),
            grad_mixed,
            preferred_element_type=jnp.float32,
        )
        grad_weights = jnp.einsum(
            "qhe,khe->hqk", grad_mixed, value_rows, preferred_element_type=jnp.float32
        )
        grad_scores = weights * (
            grad_weights - jnp.sum(grad_weights * weights, axis=-1, keepdims=True)
        )
        grad_scores = grad_scores.astype(jnp.bfloat16)
        grad_query = (
            jnp.einsum("hqk,khe->qhe", grad_scores, key_rows, preferred_element_type=jnp.float32)
            * 0.125
        )
        grad_keys = (
            grad_keys
            + jnp.einsum("hqk,qhe->khe", grad_scores, queries, preferred_element_type=jnp.float32)
            * 0.125
        )
        return ((grad_keys, grad_values), grad_query)

    zeros_kv = jnp.zeros(key_rows.shape, jnp.float32)
    (grad_keys, grad_values), grad_queries = lax.scan(
        one_block, (zeros_kv, zeros_kv), jnp.arange(blocks, dtype=jnp.int32)
    )
    return (
        grad_queries.reshape(length, -1),
        grad_keys.reshape(length, -1),
        grad_values.reshape(length, -1),
    )


def layer_forward(hidden, weights, doc_row):
    (
        pre_gain,
        pre_shift,
        qkv_weight,
        query_bias,
        value_bias,
        out_weight,
        out_bias,
        post_gain,
        post_shift,
        up_weight,
        up_bias,
        down_weight,
        down_bias,
    ) = weights
    rows_here = hidden.shape[0]
    normed = norm(hidden, pre_gain.astype(jnp.float32), pre_shift.astype(jnp.float32)).astype(
        jnp.bfloat16
    )
    bias_row = jnp.concatenate([query_bias, jnp.zeros_like(query_bias), value_bias]).astype(
        jnp.float32
    )
    packed = (project(normed, qkv_weight) + bias_row).astype(jnp.bfloat16)
    shaped = packed.reshape(rows_here, 3, HEADS, HEAD)
    mixed, log_totals = attention_forward(shaped[:, 0], shaped[:, 1], shaped[:, 2], doc_row)
    middle = hidden + project(mixed, out_weight) + out_bias.astype(jnp.float32)
    normed_two = norm(middle, post_gain.astype(jnp.float32), post_shift.astype(jnp.float32)).astype(
        jnp.bfloat16
    )
    pre_act = project(normed_two, up_weight) + up_bias.astype(jnp.float32)
    activ = gelu_tanh(pre_act).astype(jnp.bfloat16)
    output = middle + project(activ, down_weight) + down_bias.astype(jnp.float32)
    stored = (hidden, normed, packed, mixed, log_totals, middle, normed_two, pre_act, activ)
    return (output, stored)


def layer_backward(grad_out, weights, stored, doc_row):
    (
        pre_gain,
        pre_shift,
        qkv_weight,
        query_bias,
        value_bias,
        out_weight,
        out_bias,
        post_gain,
        post_shift,
        up_weight,
        up_bias,
        down_weight,
        down_bias,
    ) = weights
    hidden, normed, packed, mixed, log_totals, middle, normed_two, pre_act, activ = stored
    rows_here, width = hidden.shape
    grad_down = grad_out.astype(jnp.bfloat16)
    activ_columns = lax.all_to_all(activ, "shard", split_axis=1, concat_axis=0, tiled=True)
    group_grads = lax.all_gather(grad_down, "shard", axis=0, tiled=True)
    grad_down_weight = project_back(activ_columns, group_grads)
    width_part = width // lax.axis_size("shard")
    column_total = jnp.sum(group_grads.astype(jnp.float32), axis=0)
    grad_down_bias = lax.dynamic_slice_in_dim(
        column_total, lax.axis_index("shard") * width_part, width_part, 0
    )
    grad_activ = project_trans(grad_down, down_weight)
    unused_gelu, gelu_pull = jax.vjp(gelu_tanh, pre_act)
    grad_pre = gelu_pull(grad_activ)[0].astype(jnp.bfloat16)
    grad_up_weight = project_back(normed_two, grad_pre)
    grad_up_bias = jnp.sum(grad_pre.astype(jnp.float32), axis=0)
    grad_normed_two = project_trans(grad_pre, up_weight)
    unused_post, post_pull = jax.vjp(
        norm, middle, post_gain.astype(jnp.float32), post_shift.astype(jnp.float32)
    )
    grad_middle, grad_post_gain, grad_post_shift = post_pull(grad_normed_two)
    grad_middle = grad_middle + grad_out
    grad_attn = grad_middle.astype(jnp.bfloat16)
    grad_out_weight = project_back(mixed, grad_attn)
    grad_out_bias = jnp.sum(grad_attn.astype(jnp.float32), axis=0)
    grad_mixed = (
        project_trans(grad_attn, out_weight).astype(jnp.bfloat16).reshape(rows_here, HEADS, HEAD)
    )
    shaped = packed.reshape(rows_here, 3, HEADS, HEAD)
    grad_queries, grad_keys, grad_values = attention_backward(
        shaped[:, 0], shaped[:, 1], shaped[:, 2], doc_row, log_totals, grad_mixed
    )
    grad_packed = jnp.concatenate([grad_queries, grad_keys, grad_values], axis=1).astype(
        jnp.bfloat16
    )
    grad_qkv_weight = project_back(normed, grad_packed)
    column_sums = jnp.sum(grad_packed.astype(jnp.float32), axis=0)
    grad_query_bias = column_sums[:width]
    grad_value_bias = column_sums[2 * width :]
    grad_normed = project_trans(grad_packed, qkv_weight)
    unused_pre, pre_pull = jax.vjp(
        norm, hidden, pre_gain.astype(jnp.float32), pre_shift.astype(jnp.float32)
    )
    grad_hidden, grad_pre_gain, grad_pre_shift = pre_pull(grad_normed)
    grads = (
        grad_pre_gain,
        grad_pre_shift,
        grad_qkv_weight,
        grad_query_bias,
        grad_value_bias,
        grad_out_weight,
        grad_out_bias,
        grad_post_gain,
        grad_post_shift,
        grad_up_weight,
        grad_up_bias,
        grad_down_weight,
        grad_down_bias,
    )
    return (grad_hidden + grad_middle, grads)


def on_device(
    hidden_in,
    doc_ids,
    cotangent,
    pre_gain,
    pre_shift,
    qkv_weight,
    query_bias,
    value_bias,
    out_weight,
    out_bias,
    post_gain,
    post_shift,
    up_weight,
    up_bias,
    down_weight,
    down_bias,
):
    shards = (
        pre_gain,
        pre_shift,
        qkv_weight,
        query_bias,
        value_bias,
        out_weight,
        out_bias,
        post_gain,
        post_shift,
        up_weight,
        up_bias,
        down_weight,
        down_bias,
    )
    doc_row = doc_ids[0]
    hidden = hidden_in
    layer_index = 0
    weights = fetch_forward(shards, layer_index)
    hidden, stored = layer_forward(hidden, weights, doc_row)
    gathered_all = [weights]
    stored_all = [stored]
    grad_flow = cotangent
    reduced_all = [None] * LAYERS
    for layer_index in reversed(range(LAYERS)):
        weights = gathered_all[layer_index]
        grad_flow, layer_grads = layer_backward(
            grad_flow, weights, stored_all[layer_index], doc_row
        )
        rest_grads = tuple((layer_grads[member] for member in range(11)))
        rest_sums = reduce_nested_rest(rest_grads)
        down_pair = (layer_grads[11], layer_grads[12])
        down_sums = (
            lax.psum(down_pair[0].astype(jnp.bfloat16), "rep").astype(jnp.float32),
            lax.psum(down_pair[1].astype(jnp.bfloat16), "rep").astype(jnp.float32),
        )
        reduced_all[layer_index] = tuple(rest_sums) + tuple(down_sums)
    stacked = tuple((jnp.stack([reduced_all[0][member]]) for member in range(13)))
    return (
        hidden,
        grad_flow,
        stacked[0],
        stacked[1],
        stacked[2],
        stacked[3],
        stacked[4],
        stacked[5],
        stacked[6],
        stacked[7],
        stacked[8],
        stacked[9],
        stacked[10],
        stacked[11],
        stacked[12],
    )


def solution(mesh):
    in_specs = (
        P(("rep", "shard"), None),
        P(("rep", "shard"), None),
        P(("rep", "shard"), None),
        P(None, "shard"),
        P(None, "shard"),
        P(None, "shard", None),
        P(None, "shard"),
        P(None, "shard"),
        P(None, "shard", None),
        P(None, "shard"),
        P(None, "shard"),
        P(None, "shard"),
        P(None, "shard", None),
        P(None, "shard"),
        P(None, "shard", None),
        P(None, "shard"),
    )
    out_specs = (
        P(("rep", "shard"), None),
        P(("rep", "shard"), None),
        P(None, "shard"),
        P(None, "shard"),
        P(None, "shard", None),
        P(None, "shard"),
        P(None, "shard"),
        P(None, "shard", None),
        P(None, "shard"),
        P(None, "shard"),
        P(None, "shard"),
        P(None, "shard", None),
        P(None, "shard"),
        P(None, "shard", None),
        P(None, "shard"),
    )
    return jax.shard_map(
        on_device, mesh=mesh, in_specs=in_specs, out_specs=out_specs, check_vma=False
    )
```

profile of v0, /device:TPU:0, one launch (start us, length us, event | category | flops | bytes accessed | tf_op | source)
XLA Modules:
  0.0 431.4 jit_solution(6924387649990992)
XLA Ops:
  7.2 2.1 convert_element_type.231
  15.9 32.5 %all-reduce.17 = (bf16[768]{0:T(1024)(128)(2,1)S(1)}, bf16[768]{0:T(1024)(128)(2,1)S(1)}, bf16[768]{0:T(1024)(128)(2,1)S(1)}, bf16[768]{0:T(1024)(128)(2,1)S(1)}...) all-reduce(bf16[768]{0:T(1024)(128)(2,1)S(1)} %dynamic-update-slice, ...), channel_id=6, replica_groups=mesh['rep'=4,'shard'=8] {'shard'}, use_global_device_ids=true, to_apply=%add.3 | all-reduce | flops 5376 | bytes 21504 | tf_op jit(solution)/shard_map/all_gather | solution.py:56
  48.9 12.8 %all-gather.10 = bf16[1,3072]{1,0:T(2,128)(2,1)S(1)} all-gather(bf16[1,384]{1,0:T(2,128)(2,1)S(1)} %convert_element_type.256), channel_id=12, replica_groups=mesh['rep'=4,'shard'=8] {'shard'}, dimensions={1}, use_global_device_ids=true | all-gather | bytes 6912 | tf_op jit(solution)/shard_map/all_gather | solution.py:62
  61.8 2.8 fusion.11
  65.7 13.2 %all-gather.23.cloned.1.call-done = bf16[1,768,768]{2,1,0:T(8,128)(2,1)} async-done(((bf16[1,96,768]{2,1,0:T(8,128)(2,1)}), bf16[1,768,768]{2,1,0:T(8,128)(2,1)}) %all-gather.23.cloned.1.call-update) | async-done | bytes 1179664 | tf_op jit(solution)/shard_map/all_gather | solution.py:57
  78.9 1.7 fusion.56
  80.8 51.2 %all-gather.25.cloned.1.call-done = bf16[1,768,3072]{2,1,0:T(8,128)(2,1)} async-done(((bf16[1,96,3072]{2,1,0:T(8,128)(2,1)}), bf16[1,768,3072]{2,1,0:T(8,128)(2,1)}) %all-gather.25.cloned.1.call-update) | async-done | bytes 4718608 | tf_op jit(solution)/shard_map/all_gather | solution.py:61
  132.0 5.1 %multiply_convert_fusion = (bf16[128,3072]{1,0:T(8,128)(2,1)}, f32[128,3072]{1,0:T(8,128)}) fusion(f32[3072]{0:T(1024)S(1)} %bitcast.156, bf16[1,768,3072]{2,1,0:T(8,128)(2,1)} %all-gather.25.cloned.1.call-done, f32[128,768]{1,0:T(8,128)S(1)} %get-tuple-element.114, f32[768]{0:T(1024)S(1)} %convert_element_type.292, f32[768]{0:T(1024)S(1)} %convert_element_type.291, ...), kind=kOutput, calls=%fused_computation.27 | convolution fusion | flops 608403456 | bytes 7490560 | tf_op jit(solution)/shard_map/dot_general | solution.py:30
  137.1 47.0 %all-gather.27.cloned.1.call-done = bf16[1,3072,768]{2,1,0:T(8,128)(2,1)} async-done(((bf16[1,384,768]{2,1,0:T(8,128)(2,1)}), bf16[1,3072,768]{2,1,0:T(8,128)(2,1)}) %all-gather.27.cloned.1.call-update) | async-done | bytes 4718608 | tf_op jit(solution)/shard_map/all_gather | solution.py:63
  184.1 5.9 %fusion.57 = (bf16[3072]{0:T(1024)(128)(2,1)}, bf16[128,3072]{1,0:T(8,128)(2,1)S(1)}) fusion(f32[128,3072]{1,0:T(8,128)} %get-tuple-element.116, bf16[128,768]{1,0:T(8,128)(2,1)S(1)} %copy-done.17, bf16[1,3072,768]{2,1,0:T(8,128)(2,1)} %all-gather.27.cloned.1.call-done), kind=kOutput, calls=%fused_computation.109 | convolution fusion | flops 613807104 | bytes 7280640 | tf_op jit(solution)/shard_map/dot_general | solution.py:40
  190.0 2.3 multiply_reduce_fusion.1
  194.4 1.5 convolution_convert_fusion.2
  196.2 2.1 fusion.35
  198.3 1.1 copy.49
  199.4 1.3 multiply_reduce_fusion
  202.0 3.0 convolution_convert_fusion.1
  206.1 3.7 convolution_convert_fusion
  209.8 1.1 copy-done.9
  211.9 4.3 %all-to-all-start = ((bf16[128,8,384]{2,0,1:T(8,128)(2,1)}), bf16[128,8,384]{2,0,1:T(8,128)(2,1)}, u32[]{:S(2)}, u32[]{:S(2)}) async-start(bf16[128,8,384]{2,0,1:T(8,128)(2,1)} %bitcast.133), calls=%async_computation.3 | async-start | bytes 1572864 | tf_op jit(solution)/shard_map/all_to_all | solution.py:251
  217.9 1.7 convert_reduce_fusion
  221.1 4.8 %multiply_reduce_fusion.2 = (bf16[768]{0:T(1024)(128)(2,1)}, f32[128]{0:T(128)}, bf16[768]{0:T(1024)(128)(2,1)}, f32[128,768]{1,0:T(8,128)}) fusion(f32[128,768]{1,0:T(8,128)S(1)} %copy-done, f32[128]{0:T(128)} %copy-done.31, f32[128]{0:T(128)S(1)} %copy-done.28, f32[768]{0:T(1024)S(1)} %convert_element_type.288, ...), kind=kOutput, calls=%fused_computation.57 | convolution fusion | flops 455539072 | bytes 4922880 | tf_op jit(solution)/shard_map/dot_general | solution.py:40
  225.9 35.2 %all-reduce.16 = (bf16[768]{0:T(1024)(128)(2,1)S(1)}, bf16[768]{0:T(1024)(128)(2,1)S(1)}, bf16[768]{0:T(1024)(128)(2,1)S(1)}, bf16[768]{0:T(1024)(128)(2,1)S(1)}...) all-reduce(bf16[768]{0:T(1024)(128)(2,1)} %copy-done.38, ...), channel_id=14, replica_groups=mesh['rep'=4,'shard'=8] {'shard'}, use_global_device_ids=true, to_apply=%add.7 | all-reduce | flops 9216 | bytes 36864
  261.2 2.8 fusion.24
  264.0 32.5 %reduce-scatter.4.cloned.1.call-done = bf16[96,2304]{1,0:T(8,128)(2,1)} async-done(((bf16[768,2304]{1,0:T(8,128)(2,1)}), bf16[96,2304]{1,0:T(8,128)(2,1)}) %reduce-scatter.4.cloned.1.call-update) | async-done | bytes 442384 | tf_op jit(solution)/shard_map/reduce_scatter | solution.py:76
  296.5 55.8 %reduce-scatter.8.cloned.1.call-done = bf16[96,3072]{1,0:T(8,128)(2,1)} async-done(((bf16[768,3072]{1,0:T(8,128)(2,1)}), bf16[96,3072]{1,0:T(8,128)(2,1)}) %reduce-scatter.8.cloned.1.call-update) | async-done | bytes 589840 | tf_op jit(solution)/shard_map/reduce_scatter | solution.py:97
  352.6 10.1 %all-reduce.18 = (bf16[1,96]{1,0:T(2,128)(2,1)S(1)}, bf16[1,96]{1,0:T(2,128)(2,1)S(1)}, bf16[1,96]{1,0:T(2,128)(2,1)S(1)}, bf16[1,96]{1,0:T(2,128)(2,1)S(1)}, bf...) all-reduce(bf16[1,96]{1,0:T(2,128)(2,1)S(1)} %dynamic-slice_bitcast, ...), channel_id=1, replica_groups=mesh['rep'=4,'shard'=8] {'rep'}, use_global_device_ids=true, to_apply=%region_13.14 | all-reduce | flops 1152 | bytes 4608 | tf_op jit(solution)/shard_map/psum | solution.py:105
  368.6 3.9 fusion.29
  372.5 46.5 %all-reduce.22.cloned.1.call-done = (bf16[1,96,2304]{2,1,0:T(8,128)(2,1)}, bf16[1,96,768]{2,1,0:T(8,128)(2,1)}, bf16[1,96,3072]{2,1,0:T(8,128)(2,1)}, bf16[1,384,768]{2,1,0:T(8,128)(2,1)}) async-done(((bf16[1,96,2304]{2,1,0:T(8,128)(2,1)}, bf16[1,96,768]{2,1,0:T(8,128)(2,1)}, bf16[1,96,3072]{2,1,0:T(8,128)(2,1)}, bf16[1,384,768]{2,1,0:T(8,128)(2,1)}), (bf16[1,96,2304]{2,1,0:T(8,128)(2,1)}, ...) | async-done | bytes 1769488 | tf_op jit(solution)/shard_map/psum | solution.py:107
  419.0 2.1 stack.83
  421.1 1.6 stack.89
  422.7 1.1 stack.97
  423.8 1.1 stack.101
  (216 shorter events, 21.1 us)
Async XLA Ops:
  7.2 54.6 %all-gather.21.cloned.1.call-start = ((), (), s32[]{:S(2)}) async-start(), calls=%async_computation.8 | async-start | bytes 3981312 | tf_op jit(solution)/shard_map/all_gather | solution.py:54
  9.4 69.5 %all-gather.23.cloned.1.call-start = ((), (), s32[]{:S(2)}) async-start(), calls=%async_computation.9 | async-start | bytes 1327104 | tf_op jit(solution)/shard_map/all_gather | solution.py:57
  10.1 121.9 %all-gather.25.cloned.1.call-start = ((), (), s32[]{:S(2)}) async-start(), calls=%async_computation.10 | async-start | bytes 5308416 | tf_op jit(solution)/shard_map/all_gather | solution.py:61
  11.2 37.2 %copy-start = (f32[128,768]{1,0:T(8,128)S(1)}, f32[128,768]{1,0:T(8,128)}, u32[]{:S(2)}) copy-start(f32[128,768]{1,0:T(8,128)} %param.16) | copy-start | bytes 1179652
  11.2 172.9 %all-gather.27.cloned.1.call-start = ((), (), s32[]{:S(2)}) async-start(), calls=%async_computation.11 | async-start | bytes 5308416 | tf_op jit(solution)/shard_map/all_gather | solution.py:63
  12.1 36.7 %copy-start.41 = (s32[1,128]{1,0:T(1,128)S(1)}, s32[1,128]{1,0:T(1,128)}, u32[]{:S(2)}) copy-start(s32[1,128]{1,0:T(1,128)} %param.17) | copy-start | bytes 1540
  12.1 36.8 %copy-start.43 = (f32[1,384]{1,0:T(1,128)S(1)}, f32[1,384]{1,0:T(1,128)}, u32[]{:S(2)}) copy-start(f32[1,384]{1,0:T(1,128)} %param.29) | copy-start | bytes 4612
  12.2 205.7 %all-gather.19.cloned.1.call-start = ((), (), s32[]{:S(2)}) async-start(), calls=%async_computation.7 | async-start | bytes 1769472 | tf_op jit(solution)/shard_map/all_gather | solution.py:252
  12.9 251.1 %reduce-scatter.6.cloned.1.call-start = ((), (), s32[]{:S(2)}) async-start(), calls=%async_computation.5 | async-start | bytes 1327104 | tf_op jit(solution)/shard_map/reduce_scatter | solution.py:85
  48.4 13.4 %copy-start.22 = (f32[768]{0:T(1024)}, f32[768]{0:T(1024)S(1)}, u32[]{:S(2)}) copy-start(f32[768]{0:T(1024)S(1)} %convert_element_type.289) | copy-start | bytes 9220
  48.6 16.0 %copy-start.26 = (f32[128]{0:T(128)}, f32[128]{0:T(128)S(1)}, u32[]{:S(2)}) copy-start(f32[128]{0:T(128)S(1)} %broadcast_multiply_fusion.1) | copy-start | bytes 1540
  48.8 15.8 %copy-start.44 = (f32[128]{0:T(128)}, f32[128]{0:T(128)S(1)}, u32[]{:S(2)}) copy-start(f32[128]{0:T(128)S(1)} %multiply_reduce_fusion.6) | copy-start | bytes 1540
  48.8 15.8 %copy-start.31 = (f32[128]{0:T(128)}, f32[128]{0:T(128)S(1)}, u32[]{:S(2)}) copy-start(f32[128]{0:T(128)S(1)} %fusion.46) | copy-start | bytes 1540
  61.7 70.3 %copy-start.24 = (f32[768]{0:T(1024)}, f32[768]{0:T(1024)S(1)}, u32[]{:S(2)}) copy-start(f32[768]{0:T(1024)S(1)} %convert_element_type.292) | copy-start | bytes 9220
  65.7 71.4 %copy-start.11 = (bf16[12,64,128]{2,1,0:T(8,128)(2,1)}, bf16[12,64,128]{2,1,0:T(8,128)(2,1)S(1)}, u32[]{:S(2)}) copy-start(bf16[12,64,128]{2,1,0:T(8,128)(2,1)S(1)} %convolution_convert_fusion.5) | copy-start | bytes 589828
  80.6 111.7 %copy-start.29 = (f32[128]{0:T(128)}, f32[128]{0:T(128)S(1)}, u32[]{:S(2)}) copy-start(f32[128]{0:T(128)S(1)} %broadcast_multiply_fusion) | copy-start | bytes 1540
  80.8 111.5 %copy-start.34 = (f32[128]{0:T(128)}, f32[128]{0:T(128)S(1)}, u32[]{:S(2)}) copy-start(f32[128]{0:T(128)S(1)} %fusion.47) | copy-start | bytes 1540
  132.0 52.1 %copy-start.17 = (bf16[128,768]{1,0:T(8,128)(2,1)S(1)}, bf16[128,768]{1,0:T(8,128)(2,1)}, u32[]{:S(2)}) copy-start(bf16[128,768]{1,0:T(8,128)(2,1)} %convert_element_type.265) | copy-start | bytes 589828
  195.9 100.6 %reduce-scatter.4.cloned.1.call-start = ((), (), s32[]{:S(2)}) async-start(), calls=%async_computation.4 | async-start | bytes 3981312 | tf_op jit(solution)/shard_map/reduce_scatter | solution.py:76
  201.6 18.6 %copy-start.14 = (bf16[12,64,128]{2,1,0:T(8,128)(2,1)}, bf16[12,64,128]{2,1,0:T(8,128)(2,1)S(1)}, u32[]{:S(2)}) copy-start(bf16[12,64,128]{2,1,0:T(8,128)(2,1)S(1)} %fusion.38) | copy-start | bytes 589828
  205.0 147.3 %reduce-scatter.8.cloned.1.call-start = ((), (), s32[]{:S(2)}) async-start(), calls=%async_computation.6 | async-start | bytes 5308416 | tf_op jit(solution)/shard_map/reduce_scatter | solution.py:97
  211.9 9.1 %copy-start.28 = (f32[128]{0:T(128)S(1)}, f32[128]{0:T(128)}, u32[]{:S(2)}) copy-start(f32[128]{0:T(128)} %copy-done.26) | copy-start | bytes 1540
  211.9 49.3 %all-to-all-start = ((bf16[128,8,384]{2,0,1:T(8,128)(2,1)}), bf16[128,8,384]{2,0,1:T(8,128)(2,1)}, u32[]{:S(2)}, u32[]{:S(2)}) async-start(bf16[128,8,384]{2,0,1:T(8,128)(2,1)} %bitcast.133), calls=%async_computation.3 | async-start | bytes 1572864 | tf_op jit(solution)/shard_map/all_to_all | solution.py:251
  216.3 202.7 %all-reduce.22.cloned.1.call-start = ((), (), s32[]{:S(2)}) async-start(), calls=%async_computation.12 | async-start | bytes 3538944 | tf_op jit(solution)/shard_map/psum | solution.py:107
  221.1 40.1 %copy-start.1 = (bf16[1024,768]{1,0:T(8,128)(2,1)S(1)}, bf16[1024,768]{1,0:T(8,128)(2,1)}, u32[]{:S(2)}) copy-start(bf16[1024,768]{1,0:T(8,128)(2,1)} %all-gather.19.cloned.1.call-done) | copy-start | bytes 4718596
  264.0 88.7 %copy-start.46 = (bf16[1,96]{1,0:T(2,128)(2,1)S(1)}, bf16[1,96]{1,0:T(2,128)(2,1)}, u32[]{:S(2)}) copy-start(bf16[1,96]{1,0:T(2,128)(2,1)} %convert_bitcast_fusion) | copy-start | bytes 580
  264.0 103.4 %copy-start.45 = (f32[128]{0:T(128)S(1)}, f32[128]{0:T(128)}, u32[]{:S(2)}) copy-start(f32[128]{0:T(128)} %copy-done.44) | copy-start | bytes 1540
  264.0 103.4 %copy-start.55 = (f32[128]{0:T(128)S(1)}, f32[128]{0:T(128)}, u32[]{:S(2)}) copy-start(f32[128]{0:T(128)} %get-tuple-element.69) | copy-start | bytes 1540
  264.0 103.5 %copy-start.20 = (f32[128,768]{1,0:T(8,128)S(1)}, f32[128,768]{1,0:T(8,128)}, u32[]{:S(2)}) copy-start(f32[128,768]{1,0:T(8,128)} %get-tuple-element.120) | copy-start | bytes 1179652
  264.0 103.5 %copy-start.33 = (f32[128]{0:T(128)S(1)}, f32[128]{0:T(128)}, u32[]{:S(2)}) copy-start(f32[128]{0:T(128)} %copy-done.31) | copy-start | bytes 1540
  264.0 103.7 %copy-start.40 = (f32[128]{0:T(128)S(1)}, f32[128]{0:T(128)}, u32[]{:S(2)}) copy-start(f32[128]{0:T(128)} %copy-done.39) | copy-start | bytes 1540
  352.3 16.3 %copy-start.10 = (bf16[128,3072]{1,0:T(8,128)(2,1)S(1)}, bf16[128,3072]{1,0:T(8,128)(2,1)}, u32[]{:S(2)}) copy-start(bf16[128,3072]{1,0:T(8,128)(2,1)} %get-tuple-element.115) | copy-start | bytes 2359300
  (34 other events, 75.6 us)
Sparse Core Ops, SparseCore 0:
  10.2 44.7 all-gather.20
  57.2 21.6 all-gather.22
  81.1 50.8 all-gather.24
  134.1 49.9 all-gather.26
  186.1 24.0 all-gather.18
  212.9 36.2 reduce-scatter.5
  251.5 44.9 reduce-scatter.3
  298.8 53.4 reduce-scatter.7
  356.3 62.6 all-reduce.21
where the time goes:
time: 432 us; the launch traced here: 431 us
  waiting for transfers between devices  246 us (57%)
  blocking collectives  90.6 us (21%)
  matrix products  42.4 us (10%)
  other arithmetic  20.8 us (5%)
  between operations  16.6 us (4%)
  local copies, waits for them, and re-layouts  9.89 us (2%)
  starting transfers between devices  4.9 us (1%)
    reduce_scatter x1, waiting for transfers between devices, reduce_nested_rest(): lax.psum_scatter(grads[9].astype(jnp.bfloat16), 'shard', scatter_dimensio...  55.8 us
    all_gather x1, waiting for transfers between devices, fetch_forward(): lax.all_gather(parts[9], 'shard', axis=0, tiled=True)  51.2 us
    all_gather x1, waiting for transfers between devices, fetch_forward(): lax.all_gather(parts[11], 'shard', axis=0, tiled=True)  47 us
    psum x1, waiting for transfers between devices, reduce_nested_rest(): lax.psum(owned[2].astype(jnp.bfloat16), 'rep').astype(jnp.float32)  46.5 us
    unnamed x1, blocking collectives  35.2 us
    all_gather x1, blocking collectives, fetch_forward(): lax.all_gather(parts[4], 'shard', axis=0, tiled=True)  32.5 us
    reduce_scatter x1, waiting for transfers between devices, reduce_nested_rest(): lax.psum_scatter(grads[2].astype(jnp.bfloat16), 'shard', scatter_dimensio...  32.5 us
    dot_general x4, matrix products, project_trans(): lax.dot_general(left, right, (((1,), (1,)), ((), ())), preferred_element_...  15.2 us
  transfers between devices with their start and end apart: 10, of which 6 were waited for; matrix products, arithmetic and copies ran while one was open for 14% of the time, Pallas kernels for 0%

commit v1 on v0

--- a/solution.py
+++ b/solution.py
@@ -9,6 +9,12 @@
 EPS = 1e-05
 GELU_C = 0.7978845608028654
 NEG_FILL = -1e30
+
+
+def tiled_gather(x, axis, dim):
+    count = lax.axis_size(axis)
+    repeats = [count if d == dim else 1 for d in range(x.ndim)]
+    return lax.all_to_all(jnp.tile(x, repeats), axis, split_axis=dim, concat_axis=dim, tiled=True)
 
 
 def norm(values_in, gains, shifts):
@@ -58,7 +64,7 @@
         lax.all_gather(parts[6], "shard", axis=0, tiled=True),
         lax.all_gather(parts[7], "shard", axis=0, tiled=True),
         lax.all_gather(parts[8], "shard", axis=0, tiled=True),
-        lax.all_gather(parts[9], "shard", axis=0, tiled=True),
+        tiled_gather(parts[9], "shard", 0),
         lax.all_gather(parts[10], "shard", axis=0, tiled=True),
         lax.all_gather(parts[11], "shard", axis=0, tiled=True),
         lax.all_gather(parts[12], "shard", axis=0, tiled=True),

time: 432 us -> 453 us (1.049)
  blocking collectives: 90.6 us -> 228 us
  waiting for transfers between devices: 246 us -> 118 us
  starting transfers between devices: 4.9 us -> 11.4 us
    all_gather x1, blocking collectives: 32.5 us -> 173 us  [fetch_forward(): lax.all_gather(parts[4], 'shard', axis=0, tiled=True)]
    all_gather x1 -> x0, waiting for transfers between devices: 51.2 us -> none  [fetch_forward(): lax.all_gather(parts[9], 'shard', axis=0, tiled=True)]
    all_gather x1, waiting for transfers between devices: 47 us -> 0.01 us  [fetch_forward(): lax.all_gather(parts[11], 'shard', axis=0, tiled=True)]
    reduce_scatter x1, waiting for transfers between devices: 32.5 us -> 15.3 us  [reduce_nested_rest(): lax.psum_scatter(grads[2].astype(jnp.bfloat16), 'shard', scatter_dimensio...]
    all_gather x1, waiting for transfers between devices: 13.2 us -> 0.01 us  [fetch_forward(): lax.all_gather(parts[5], 'shard', axis=0, tiled=True)]
    all_to_all x0 -> x1, starting transfers between devices: none -> 6.5 us  [tiled_gather(): lax.all_to_all(jnp.tile(x, repeats), axis, split_axis=dim, concat_axis=di...]
  transfers between devices with their start and end apart: 10 -> 10, of which waited for: 6 -> 3; matrix products, arithmetic and copies ran while one was open for 14% -> 15% of each run, Pallas kernels for 0% -> 0%
where the time goes in v1:
time: 453 us; the launch traced here: 452 us
  blocking collectives  228 us (50%)
  waiting for transfers between devices  118 us (26%)
  matrix products  45.2 us (10%)
  other arithmetic  20 us (4%)
  between operations  16.8 us (4%)
  local copies, waits for them, and re-layouts  13.4 us (3%)
  starting transfers between devices  11.4 us (3%)
    all_gather x1, blocking collectives, fetch_forward(): lax.all_gather(parts[4], 'shard', axis=0, tiled=True)  173 us
    reduce_scatter x1, waiting for transfers between devices, reduce_nested_rest(): lax.psum_scatter(grads[9].astype(jnp.bfloat16), 'shard', scatter_dimensio...  55.7 us
    psum x1, waiting for transfers between devices, reduce_nested_rest(): lax.psum(owned[2].astype(jnp.bfloat16), 'rep').astype(jnp.float32)  46.5 us
    unnamed x1, blocking collectives  31 us
    dot_general x4, matrix products, project_trans(): lax.dot_general(left, right, (((1,), (1,)), ((), ())), preferred_element_...  17.7 us
    reduce_scatter x1, waiting for transfers between devices, reduce_nested_rest(): lax.psum_scatter(grads[2].astype(jnp.bfloat16), 'shard', scatter_dimensio...  15.3 us
    all_gather x1, blocking collectives, fetch_forward(): lax.all_gather(parts[10], 'shard', axis=0, tiled=True)  13.7 us
    dot_general x4, matrix products, project(): return jnp.dot(left, right, preferred_element_type=jnp.float32)  13.5 us
  transfers between devices with their start and end apart: 10, of which 3 were waited for; matrix products, arithmetic and copies ran while one was open for 15% of the time, Pallas kernels for 0%

profile of v1, /device:TPU:0, one launch (start us, length us, event | category | flops | bytes accessed | tf_op | source)
XLA Modules:
  0.0 452.2 jit_solution(10426883077644279515)
XLA Ops:
  7.2 2.1 convert_element_type.235
  11.2 2.8 tile.2
  14.1 6.5 %all-to-all-start = ((bf16[8,96,3072]{2,1,0:T(8,128)(2,1)}), bf16[8,96,3072]{2,1,0:T(8,128)(2,1)}, u32[]{:S(2)}, u32[]{:S(2)}) async-start(bf16[8,96,3072]{2,1,0:T(8,128)(2,1)} %tile.2), calls=%async_computation | async-start | bytes 9437184 | tf_op jit(solution)/shard_map/all_to_all | solution.py:17
  24.4 172.9 %all-reduce.17 = (bf16[768]{0:T(1024)(128)(2,1)S(1)}, bf16[768]{0:T(1024)(128)(2,1)S(1)}, bf16[768]{0:T(1024)(128)(2,1)S(1)}, bf16[768]{0:T(1024)(128)(2,1)S(1)}...) all-reduce(bf16[768]{0:T(1024)(128)(2,1)S(1)} %dynamic-update-slice, ...), channel_id=6, replica_groups=mesh['rep'=4,'shard'=8] {'shard'}, use_global_device_ids=true, to_apply=%add.3 | all-reduce | flops 5376 | bytes 21504 | tf_op jit(solution)/shard_map/all_gather | solution.py:62
  197.3 13.7 %all-gather.9 = bf16[1,3072]{1,0:T(2,128)(2,1)S(1)} all-gather(bf16[1,384]{1,0:T(2,128)(2,1)S(1)} %convert_element_type.260), channel_id=11, replica_groups=mesh['rep'=4,'shard'=8] {'shard'}, dimensions={1}, use_global_device_ids=true | all-gather | bytes 6912 | tf_op jit(solution)/shard_map/all_gather | solution.py:68
  212.1 2.7 fusion.4
  215.9 1.8 fusion.49
  218.0 5.2 %multiply_convert_fusion = (bf16[128,3072]{1,0:T(8,128)(2,1)}, f32[128,3072]{1,0:T(8,128)}) fusion(f32[3072]{0:T(1024)S(1)} %bitcast.150, bf16[768,3072]{1,0:T(8,128)(2,1)} %bitcast.18, f32[128,768]{1,0:T(8,128)S(1)} %get-tuple-element.114, f32[768]{0:T(1024)S(1)} %convert_element_type.296, f32[768]{0:T(1024)S(1)} %convert_element_type.295, ...), kind=kOutput, calls=%fused_computation.23 | convolution fusion | flops 608403456 | bytes 7490560 | tf_op jit(solution)/shard_map/dot_general | solution.py:36
  223.2 5.8 %fusion.50 = (bf16[3072]{0:T(1024)(128)(2,1)}, bf16[128,3072]{1,0:T(8,128)(2,1)S(1)}) fusion(f32[128,3072]{1,0:T(8,128)} %get-tuple-element.116, bf16[128,768]{1,0:T(8,128)(2,1)S(1)} %copy-done.16, bf16[1,3072,768]{2,1,0:T(8,128)(2,1)} %all-gather.23.cloned.1.call-done), kind=kOutput, calls=%fused_computation.106 | convolution fusion | flops 613807104 | bytes 7280640 | tf_op jit(solution)/shard_map/dot_general | solution.py:46
  229.0 4.9 %multiply_reduce_fusion.1 = (bf16[768]{0:T(1024)(128)(2,1)}, f32[128]{0:T(128)S(1)}, bf16[768]{0:T(1024)(128)(2,1)}, f32[128,768]{1,0:T(8,128)S(1)}) fusion(f32[128,768]{1,0:T(8,128)S(1)} %get-tuple-element.114, f32[128]{0:T(128)S(1)} %fusion.40, f32[128]{0:T(128)S(1)} %broadcast_multiply_fusion, f32[768]{0:T(1024)S(1)} %convert_element_type.295, ...), kind=kOutput, calls=%fused_computation.53 | convolution fusion | flops 604764544 | bytes 6299136 | tf_op jit(solution)/shard_map/dot_general | solution.py:46
  236.2 1.5 convolution_convert_fusion.2
  237.9 2.1 fusion.28
  240.1 1.1 copy.49
  241.2 1.3 multiply_reduce_fusion
  243.8 3.1 convolution_convert_fusion.1
  246.9 1.1 copy-done.7
  248.0 3.7 convolution_convert_fusion
  251.7 1.1 copy-done.8
  253.8 4.3 all-to-all-start.1
  259.8 1.7 convert_reduce_fusion
  263.0 4.8 %multiply_reduce_fusion.2 = (bf16[768]{0:T(1024)(128)(2,1)}, f32[128]{0:T(128)}, bf16[768]{0:T(1024)(128)(2,1)}, f32[128,768]{1,0:T(8,128)}) fusion(f32[128,768]{1,0:T(8,128)S(1)} %copy-done, f32[128]{0:T(128)} %copy-done.30, f32[128]{0:T(128)S(1)} %copy-done.27, f32[768]{0:T(1024)S(1)} %convert_element_type.292, ...), kind=kOutput, calls=%fused_computation.54 | convolution fusion | flops 455539072 | bytes 4922880 | tf_op jit(solution)/shard_map/dot_general | solution.py:46
  267.8 31.0 %all-reduce.16 = (bf16[768]{0:T(1024)(128)(2,1)S(1)}, bf16[768]{0:T(1024)(128)(2,1)S(1)}, bf16[768]{0:T(1024)(128)(2,1)S(1)}, bf16[768]{0:T(1024)(128)(2,1)S(1)}...) all-reduce(bf16[768]{0:T(1024)(128)(2,1)} %copy-done.37, ...), channel_id=13, replica_groups=mesh['rep'=4,'shard'=8] {'shard'}, use_global_device_ids=true, to_apply=%add.7 | all-reduce | flops 9216 | bytes 36864
  298.8 2.8 fusion.17
  301.7 15.3 %reduce-scatter.4.cloned.1.call-done = bf16[96,2304]{1,0:T(8,128)(2,1)} async-done(((bf16[768,2304]{1,0:T(8,128)(2,1)}), bf16[96,2304]{1,0:T(8,128)(2,1)}) %reduce-scatter.4.cloned.1.call-update) | async-done | bytes 442384 | tf_op jit(solution)/shard_map/reduce_scatter | solution.py:82
  317.0 55.7 %reduce-scatter.8.cloned.1.call-done = bf16[96,3072]{1,0:T(8,128)(2,1)} async-done(((bf16[768,3072]{1,0:T(8,128)(2,1)}), bf16[96,3072]{1,0:T(8,128)(2,1)}) %reduce-scatter.8.cloned.1.call-update) | async-done | bytes 589840 | tf_op jit(solution)/shard_map/reduce_scatter | solution.py:103
  373.1 10.1 %all-reduce.18 = (bf16[1,96]{1,0:T(2,128)(2,1)S(1)}, bf16[1,96]{1,0:T(2,128)(2,1)S(1)}, bf16[1,96]{1,0:T(2,128)(2,1)S(1)}, bf16[1,96]{1,0:T(2,128)(2,1)S(1)}, bf...) all-reduce(bf16[1,96]{1,0:T(2,128)(2,1)S(1)} %dynamic-slice_bitcast, ...), channel_id=1, replica_groups=mesh['rep'=4,'shard'=8] {'rep'}, use_global_device_ids=true, to_apply=%region_13.14 | all-reduce | flops 1152 | bytes 4608 | tf_op jit(solution)/shard_map/psum | solution.py:111
  389.0 3.9 fusion.22
  392.9 46.5 %all-reduce.22.cloned.1.call-done = (bf16[1,96,2304]{2,1,0:T(8,128)(2,1)}, bf16[1,96,768]{2,1,0:T(8,128)(2,1)}, bf16[1,96,3072]{2,1,0:T(8,128)(2,1)}, bf16[1,384,768]{2,1,0:T(8,128)(2,1)}) async-done(((bf16[1,96,2304]{2,1,0:T(8,128)(2,1)}, bf16[1,96,768]{2,1,0:T(8,128)(2,1)}, bf16[1,96,3072]{2,1,0:T(8,128)(2,1)}, bf16[1,384,768]{2,1,0:T(8,128)(2,1)}), (bf16[1,96,2304]{2,1,0:T(8,128)(2,1)}, ...) | async-done | bytes 1769488 | tf_op jit(solution)/shard_map/psum | solution.py:113
  439.4 2.1 stack.83
  441.5 1.6 stack.89
  443.1 1.1 stack.97
  444.3 1.1 stack.101
  (214 shorter events, 19.9 us)
Async XLA Ops:
  7.2 204.9 %all-gather.19.cloned.1.call-start = ((), (), s32[]{:S(2)}) async-start(), calls=%async_computation.9 | async-start | bytes 3981312 | tf_op jit(solution)/shard_map/all_gather | solution.py:60
  9.4 206.6 %all-gather.21.cloned.1.call-start = ((), (), s32[]{:S(2)}) async-start(), calls=%async_computation.10 | async-start | bytes 1327104 | tf_op jit(solution)/shard_map/all_gather | solution.py:63
  10.1 213.0 %all-gather.23.cloned.1.call-start = ((), (), s32[]{:S(2)}) async-start(), calls=%async_computation.11 | async-start | bytes 5308416 | tf_op jit(solution)/shard_map/all_gather | solution.py:69
  14.0 9.0 %copy-start.47 = (f32[1,96]{1,0:T(1,128)S(1)}, f32[1,96]{1,0:T(1,128)}, u32[]{:S(2)}) copy-start(f32[1,96]{1,0:T(1,128)} %param.22) | copy-start | bytes 1156
  14.0 9.2 %copy-start.48 = (f32[1,96]{1,0:T(1,128)S(1)}, f32[1,96]{1,0:T(1,128)}, u32[]{:S(2)}) copy-start(f32[1,96]{1,0:T(1,128)} %param.20) | copy-start | bytes 1156
  14.0 9.4 %copy-start.49 = (f32[1,96]{1,0:T(1,128)S(1)}, f32[1,96]{1,0:T(1,128)}, u32[]{:S(2)}) copy-start(f32[1,96]{1,0:T(1,128)} %param.19) | copy-start | bytes 1156
  14.0 9.7 %copy-start.50 = (f32[1,96]{1,0:T(1,128)S(1)}, f32[1,96]{1,0:T(1,128)}, u32[]{:S(2)}) copy-start(f32[1,96]{1,0:T(1,128)} %param.25) | copy-start | bytes 1156
  14.0 9.9 %copy-start.51 = (f32[1,96]{1,0:T(1,128)S(1)}, f32[1,96]{1,0:T(1,128)}, u32[]{:S(2)}) copy-start(f32[1,96]{1,0:T(1,128)} %param.27) | copy-start | bytes 1156
  14.0 10.1 %copy-start.52 = (f32[1,96]{1,0:T(1,128)S(1)}, f32[1,96]{1,0:T(1,128)}, u32[]{:S(2)}) copy-start(f32[1,96]{1,0:T(1,128)} %param.26) | copy-start | bytes 1156
  14.0 183.3 %copy-start.42 = (f32[1,384]{1,0:T(1,128)S(1)}, f32[1,384]{1,0:T(1,128)}, u32[]{:S(2)}) copy-start(f32[1,384]{1,0:T(1,128)} %param.29) | copy-start | bytes 4612
  14.0 197.0 %copy-start = (f32[128,768]{1,0:T(8,128)S(1)}, f32[128,768]{1,0:T(8,128)}, u32[]{:S(2)}) copy-start(f32[128,768]{1,0:T(8,128)} %param.16) | copy-start | bytes 1179652
  14.1 203.9 %all-to-all-start = ((bf16[8,96,3072]{2,1,0:T(8,128)(2,1)}), bf16[8,96,3072]{2,1,0:T(8,128)(2,1)}, u32[]{:S(2)}, u32[]{:S(2)}) async-start(bf16[8,96,3072]{2,1,0:T(8,128)(2,1)} %tile.2), calls=%async_computation | async-start | bytes 9437184 | tf_op jit(solution)/shard_map/all_to_all | solution.py:17
  20.6 191.4 %copy-start.40 = (s32[1,128]{1,0:T(1,128)S(1)}, s32[1,128]{1,0:T(1,128)}, u32[]{:S(2)}) copy-start(s32[1,128]{1,0:T(1,128)} %param.17) | copy-start | bytes 1540
  20.6 239.2 %all-gather.17.cloned.1.call-start = ((), (), s32[]{:S(2)}) async-start(), calls=%async_computation.8 | async-start | bytes 1769472 | tf_op jit(solution)/shard_map/all_gather | solution.py:258
  21.3 280.3 %reduce-scatter.6.cloned.1.call-start = ((), (), s32[]{:S(2)}) async-start(), calls=%async_computation.6 | async-start | bytes 1327104 | tf_op jit(solution)/shard_map/reduce_scatter | solution.py:91
  197.3 17.5 %copy-start.21 = (f32[768]{0:T(1024)}, f32[768]{0:T(1024)S(1)}, u32[]{:S(2)}) copy-start(f32[768]{0:T(1024)S(1)} %convert_element_type.293) | copy-start | bytes 9220
  217.8 16.2 %copy-start.28 = (f32[128]{0:T(128)}, f32[128]{0:T(128)S(1)}, u32[]{:S(2)}) copy-start(f32[128]{0:T(128)S(1)} %broadcast_multiply_fusion) | copy-start | bytes 1540
  218.0 16.0 %copy-start.33 = (f32[128]{0:T(128)}, f32[128]{0:T(128)S(1)}, u32[]{:S(2)}) copy-start(f32[128]{0:T(128)S(1)} %fusion.40) | copy-start | bytes 1540
  237.7 79.3 %reduce-scatter.4.cloned.1.call-start = ((), (), s32[]{:S(2)}) async-start(), calls=%async_computation.5 | async-start | bytes 3981312 | tf_op jit(solution)/shard_map/reduce_scatter | solution.py:82
  243.3 18.8 %copy-start.13 = (bf16[12,64,128]{2,1,0:T(8,128)(2,1)}, bf16[12,64,128]{2,1,0:T(8,128)(2,1)S(1)}, u32[]{:S(2)}) copy-start(bf16[12,64,128]{2,1,0:T(8,128)(2,1)S(1)} %fusion.31) | copy-start | bytes 589828
  246.9 125.9 %reduce-scatter.8.cloned.1.call-start = ((), (), s32[]{:S(2)}) async-start(), calls=%async_computation.7 | async-start | bytes 5308416 | tf_op jit(solution)/shard_map/reduce_scatter | solution.py:103
  253.8 9.1 %copy-start.27 = (f32[128]{0:T(128)S(1)}, f32[128]{0:T(128)}, u32[]{:S(2)}) copy-start(f32[128]{0:T(128)} %copy-done.25) | copy-start | bytes 1540
  253.8 45.0 %all-to-all-start.1 = ((bf16[128,8,384]{2,0,1:T(8,128)(2,1)}), bf16[128,8,384]{2,0,1:T(8,128)(2,1)}, u32[]{:S(2)}, u32[]{:S(2)}) async-start(bf16[128,8,384]{2,0,1:T(8,128)(2,1)} %bitcast.127), calls=%async_computation.4 | async-start | bytes 1572864 | tf_op jit(solution)/shard_map/all_to_all | solution.py:257
  258.2 181.2 %all-reduce.22.cloned.1.call-start = ((), (), s32[]{:S(2)}) async-start(), calls=%async_computation.12 | async-start | bytes 3538944 | tf_op jit(solution)/shard_map/psum | solution.py:113
  263.0 35.9 %copy-start.1 = (bf16[1024,768]{1,0:T(8,128)(2,1)S(1)}, bf16[1024,768]{1,0:T(8,128)(2,1)}, u32[]{:S(2)}) copy-start(bf16[1024,768]{1,0:T(8,128)(2,1)} %all-gather.17.cloned.1.call-done) | copy-start | bytes 4718596
  301.6 71.5 %copy-start.45 = (bf16[1,96]{1,0:T(2,128)(2,1)S(1)}, bf16[1,96]{1,0:T(2,128)(2,1)}, u32[]{:S(2)}) copy-start(bf16[1,96]{1,0:T(2,128)(2,1)} %convert_bitcast_fusion.1) | copy-start | bytes 580
  301.6 86.2 %copy-start.44 = (f32[128]{0:T(128)S(1)}, f32[128]{0:T(128)}, u32[]{:S(2)}) copy-start(f32[128]{0:T(128)} %copy-done.43) | copy-start | bytes 1540
  301.6 86.2 %copy-start.54 = (f32[128]{0:T(128)S(1)}, f32[128]{0:T(128)}, u32[]{:S(2)}) copy-start(f32[128]{0:T(128)} %get-tuple-element.69) | copy-start | bytes 1540
  301.6 86.2 %copy-start.19 = (f32[128,768]{1,0:T(8,128)S(1)}, f32[128,768]{1,0:T(8,128)}, u32[]{:S(2)}) copy-start(f32[128,768]{1,0:T(8,128)} %get-tuple-element.120) | copy-start | bytes 1179652
  301.6 86.2 %copy-start.32 = (f32[128]{0:T(128)S(1)}, f32[128]{0:T(128)}, u32[]{:S(2)}) copy-start(f32[128]{0:T(128)} %copy-done.30) | copy-start | bytes 1540
  301.6 86.5 %copy-start.39 = (f32[128]{0:T(128)S(1)}, f32[128]{0:T(128)}, u32[]{:S(2)}) copy-start(f32[128]{0:T(128)} %copy-done.38) | copy-start | bytes 1540
  372.8 16.2 %copy-start.9 = (bf16[128,3072]{1,0:T(8,128)(2,1)S(1)}, bf16[128,3072]{1,0:T(8,128)(2,1)}, u32[]{:S(2)}) copy-start(bf16[128,3072]{1,0:T(8,128)(2,1)} %get-tuple-element.115) | copy-start | bytes 2359300
  (33 other events, 104.6 us)
Sparse Core Ops, SparseCore 0:
  10.2 72.3 all-gather.18
  84.8 60.3 all-gather.20
  147.4 56.1 all-gather.22
  205.7 24.0 all-gather.16
  237.8 32.7 reduce-scatter.5
  272.8 44.1 reduce-scatter.3
  319.3 53.3 reduce-scatter.7
  376.8 62.6 all-reduce.21
